TPU v7x, 256 devices: a whole 4x4x8 slice. The times are simulated.
256 devices in a mesh: seq: 64 (over x, z, core), head: 4 (over y).
Axes of the slice: x: 4, y: 4, z: 8, core: 2. Of those that a mesh axis runs over, the one named last changes fastest.
Arguments:
- tokens: bfloat16 [65536, 2048], P('seq', 'head'), may hold values from -6 to 6
- w_qkv: bfloat16 [2048, 6144], P(None, 'head'), may hold values from -1 to 1
- item_at: int32 [4, 2048], P('head'), may hold values from 0 to 2047, as said below
- rand_cols: int32 [16, 512, 4], P('head'), may hold values from 0 to 511, as said below
- rand_used: int32 [16, 512], P('head'), may hold values from 0 to 4, as said below
Outputs:
- attended: bfloat16 [4, 2048, 128, 128], P('head', 'seq')
Inputs may be any that keep to these rules, and one draw needn't show every extreme that they name: In head group g, item e * 512 + r stands for head g * 4 + e at block row r, and every item appears exactly once in item_at[g]. Positions j * 32 to (j + 1) * 32 - 1 hold the items placed at device j of seq. Of the items whose block rows lie on one device of seq, at most 1 of one group are placed at any one device, and exactly 1 at some. `rand_cols`: take all 128 candidates (used or not) of the items placed at one device in one head group, or of the items of one group whose block rows lie on one device: at most 2 of them lie in the block rows of any one device of seq, and exactly 2 in some. A candidate may equal a window block or block 0. `rand_used`: in each head group the counts of the 32 items placed at one device sum to exactly 64; the sums over the items whose block rows lie on one device vary.
All inputs are finite; a program needn't handle non-finite values.
Results may differ from a plain program's by a relative error of at most 0.019.
Values may be sent and summed in bfloat16 or wider, within the bound.
No kernel may reach another device: no remote copies, remote signals or barrier semaphores. Data moves between devices by JAX's collectives and lax.ppermute only.
A program may use at most 128 MiB of HBM per device.

v0:
```python
import math
import jax
import jax.numpy as jnp
from jax import lax
from jax.sharding import PartitionSpec as P

neg_large = -1e30


def extended(block, sides, width):
    for axis, dim in sides:
        count = lax.axis_size(axis)
        forward = [(i, i + 1) for i in range(count - 1)]
        backward = [(target, source) for source, target in forward]
        low = lax.ppermute(
            lax.slice_in_dim(block, block.shape[dim] - width, None, axis=dim), axis, forward
        )
        high = lax.ppermute(lax.slice_in_dim(block, 0, width, axis=dim), axis, backward)
        block = jnp.concatenate([low, block, high], axis=dim)
    return block


def broadcast(block, axis, owner):
    block = jnp.where(lax.axis_index(axis) == owner, block, jnp.zeros_like(block))
    return lax.psum(block, axis)


def packed_attend(
    queries, near_keys, near_values, near_usable, rand_keys, rand_values, slot_item, factor
):
    item_count = queries.shape[0]
    near_scores = (
        jnp.einsum("ibe,ijke->ibjk", queries, near_keys, preferred_element_type=jnp.float32)
        * factor
    )
    near_scores = jnp.where(near_usable[:, None, :, None], near_scores, neg_large)
    rand_scores = (
        jnp.einsum(
            "kbe,kce->kbc", queries[slot_item], rand_keys, preferred_element_type=jnp.float32
        )
        * factor
    )
    member = slot_item[None, :] == jnp.arange(item_count, dtype=jnp.int32)[:, None]
    slot_max = jnp.max(rand_scores, axis=2)
    rand_max = jnp.max(jnp.where(member[:, :, None], slot_max[None], neg_large), axis=1)
    row_max = jnp.maximum(jnp.max(near_scores, axis=(2, 3)), rand_max)
    near_expo = jnp.exp(near_scores - row_max[:, :, None, None])
    rand_expo = jnp.exp(rand_scores - row_max[slot_item][:, :, None])
    slot_total = jnp.sum(rand_expo, axis=2)
    row_sum = jnp.sum(near_expo, axis=(2, 3)) + jnp.sum(
        jnp.where(member[:, :, None], slot_total[None], 0.0), axis=1
    )
    summed = jnp.einsum(
        "ibjk,ijke->ibe",
        near_expo.astype(jnp.bfloat16),
        near_values,
        preferred_element_type=jnp.float32,
    )
    slot_out = jnp.einsum(
        "kbc,kce->kbe",
        rand_expo.astype(jnp.bfloat16),
        rand_values,
        preferred_element_type=jnp.float32,
    )
    summed = summed + jnp.einsum(
        "ik,kbe->ibe", member.astype(jnp.float32), slot_out, precision=lax.Precision.HIGHEST
    )
    return (summed, row_max, row_sum)


def rank_among(homes):
    count = homes.shape[-1]
    earlier = jnp.tril(jnp.ones((count, count), bool), -1)
    same_home = homes[..., :, None] == homes[..., None, :]
    return jnp.sum(same_home & earlier, axis=-1)


def pack_live(counts, rand_count, live_total):
    slot_total = counts.shape[0] * rand_count
    slot_ids = jnp.arange(slot_total, dtype=jnp.int32)
    live = slot_ids % rand_count < jnp.repeat(counts, rand_count)
    live_rank = jnp.cumsum(live.astype(jnp.int32)) - 1
    picks = live[:, None] & (live_rank[:, None] == jnp.arange(live_total, dtype=jnp.int32)[None, :])
    return jnp.sum(jnp.where(picks, slot_ids[:, None], 0), axis=0)


def local(tokens, w_qkv, item_at, rand_cols, rand_used):
    seq_count = lax.axis_size("seq")
    my_seq = lax.axis_index("seq")
    heads_dev, nblocks, rand_count = rand_cols.shape
    tokens_dev = tokens.shape[0]
    head_dim = w_qkv.shape[1] // (3 * heads_dev)
    block_len = tokens_dev * seq_count // nblocks
    rows_dev = tokens_dev // block_len
    items_dev = heads_dev * rows_dev
    slot_count = items_dev * rand_count
    live_total = slot_count // 2
    cap_items = max(1, items_dev // seq_count)
    cap_tiles = max(1, slot_count // seq_count)
    factor = 1.0 / math.sqrt(head_dim)
    projected = jnp.dot(
        lax.all_gather(tokens, "head", axis=1, tiled=True),
        w_qkv,
        preferred_element_type=jnp.float32,
    )
    projected = projected.astype(jnp.bfloat16).reshape(rows_dev, block_len, 3, heads_dev, head_dim)
    query_tiles = projected[:, :, 0].transpose(2, 0, 1, 3).reshape(items_dev, block_len, head_dim)
    pair_rows = projected[:, :, 1:].reshape(tokens_dev, 2, heads_dev, head_dim)
    widened = extended(pair_rows, (("seq", 0),), block_len)
    pair_tiles = widened.reshape(rows_dev + 2, block_len, 2, heads_dev, head_dim).transpose(
        3, 0, 2, 1, 4
    )
    own_tiles = pair_tiles[:, 1 : rows_dev + 1].reshape(items_dev, 2, block_len, head_dim)
    first_tiles = broadcast(pair_tiles[:, 1], "seq", 0)
    window_tiles = jnp.stack(
        [
            pair_tiles[:, 0:rows_dev],
            pair_tiles[:, 1 : rows_dev + 1],
            pair_tiles[:, 2 : rows_dev + 2],
        ],
        axis=2,
    )
    window_tiles = window_tiles.reshape(items_dev, 3, 2, block_len, head_dim)
    placed = item_at[0].reshape(seq_count, items_dev)
    placed_head = placed // nblocks
    placed_row = placed % nblocks
    placed_home = placed_row // rows_dev
    local_index = placed_head * rows_dev + placed_row % rows_dev
    is_mine = placed_home == my_seq
    rank_mine = jnp.cumsum(is_mine.astype(jnp.int32), axis=1) - 1
    slot_ids = jnp.arange(cap_items, dtype=jnp.int32)
    slot_hit = is_mine[:, :, None] & (rank_mine[:, :, None] == slot_ids)
    send_index = jnp.sum(jnp.where(slot_hit, local_index[:, :, None], 0), axis=1).reshape(-1)
    my_items = lax.dynamic_index_in_dim(placed, my_seq, 0, keepdims=False)
    item_head = my_items // nblocks
    item_row = my_items % nblocks
    item_home = item_row // rows_dev
    recv_slot = item_home * cap_items + rank_among(item_home)
    my_random = rand_cols[item_head, item_row].reshape(-1)
    tile_home = my_random // rows_dev
    tile_rank = rank_among(tile_home)
    tile_slot = tile_home * cap_tiles + tile_rank
    tile_ids = jnp.arange(cap_tiles, dtype=jnp.int32)
    peer_ids = jnp.arange(seq_count, dtype=jnp.int32)
    slot_head = jnp.repeat(item_head, rand_count)
    tile_local = slot_head * rows_dev + my_random % rows_dev
    wanted = (tile_home[None, :, None] == peer_ids[:, None, None]) & (
        tile_rank[None, :, None] == tile_ids[None, None, :]
    )
    requests = jnp.sum(jnp.where(wanted, tile_local[None, :, None], 0), axis=1)
    asked = lax.all_to_all(requests, "seq", split_axis=0, concat_axis=0, tiled=True)
    picked = own_tiles[asked.reshape(-1)].reshape(asked.shape + own_tiles.shape[1:])
    fetched = lax.all_to_all(picked, "seq", split_axis=0, concat_axis=0, tiled=True)
    gathered = fetched.reshape(seq_count * cap_tiles, 2, block_len, head_dim)[tile_slot]
    random_tiles = gathered.reshape(items_dev, rand_count, 2, block_len, head_dim)
    item_counts = rand_used[item_head, item_row]
    live_slots = pack_live(item_counts, rand_count, live_total)
    packed_tiles = random_tiles.reshape(slot_count, 2, block_len, head_dim)[live_slots]
    slot_item = live_slots // rand_count
    global_tiles = first_tiles[item_head][:, None]
    sent_query = query_tiles[send_index].reshape(seq_count, cap_items, block_len, head_dim)
    sent_window = window_tiles[send_index].reshape(seq_count, cap_items, 3, 2, block_len, head_dim)
    got_query, got_window = (
        lax.all_to_all(sent_query, "seq", split_axis=0, concat_axis=0, tiled=True),
        lax.all_to_all(sent_window, "seq", split_axis=0, concat_axis=0, tiled=True),
    )
    queries = got_query.reshape(seq_count * cap_items, block_len, head_dim)[recv_slot]
    windows = got_window.reshape(seq_count * cap_items, 3, 2, block_len, head_dim)[recv_slot]
    near_tiles = jnp.concatenate([windows, global_tiles], axis=1)
    near_usable = jnp.concatenate(
        [
            (item_row >= 1)[:, None],
            jnp.ones((items_dev, 1), bool),
            (item_row + 1 < nblocks)[:, None],
            jnp.ones((items_dev, 1), bool),
        ],
        axis=1,
    )
    summed, row_max, row_sum = packed_attend(
        queries,
        near_tiles[:, :, 0],
        near_tiles[:, :, 1],
        near_usable,
        packed_tiles[:, 0],
        packed_tiles[:, 1],
        slot_item,
        factor,
    )
    result = (summed / row_sum[:, :, None]).astype(jnp.bfloat16)
    return result.reshape(1, items_dev, block_len, head_dim)


def solution(mesh):
    return jax.shard_map(
        local,
        mesh=mesh,
        in_specs=(
            P("seq", "head"),
            P(None, "head"),
            P("head", None),
            P("head", None, None),
            P("head", None),
        ),
        out_specs=P("head", "seq", None, None),
        check_vma=False,
    )
```

profile of v0, /device:TPU:1, one launch (start us, length us, event | category | flops | bytes accessed | tf_op | source)
XLA Modules:
  0.0 679.1 jit_solution(8968216010016144075)
XLA Ops:
  6.5 0.7 all-gather.2.cloned.1.call-update
  7.3 0.5 broadcast.1180
  7.8 1.3 reduce.15
  9.2 1.1 copy.117
  10.4 0.2 convert_reduce_fusion.1
  10.6 0.6 fusion.78
  11.2 0.7 gather_fusion.7
  12.2 0.2 convert_reduce_fusion
  12.5 0.7 copy.118
  13.3 13.0 %all-to-all-start.2 = ((s32[64,1,2]{2,1,0:T(1,128)}), s32[64,1,2]{2,1,0:T(1,128)S(1)}, u32[]{:S(2)}, u32[]{:S(2)}) async-start(s32[64,1,2]{2,1,0:T(1,128)} %copy.118), calls=%async_computation.2 | async-start | bytes 65536 | tf_op jit(solution)/shard_map/all_to_all | solution.py:151
  26.3 0.2 reduce_window_sum.18
  26.5 0.8 reshape_squeeze.6
  27.5 36.4 %all-gather.2.cloned.1.call-done = bf16[1024,2048]{1,0:T(8,128)(2,1)} async-done(((bf16[1024,512]{1,0:T(8,128)(2,1)}), bf16[1024,2048]{1,0:T(8,128)(2,1)}) %all-gather.2.cloned.1.call-update) | async-done | bytes 4194320 | tf_op jit(solution)/shard_map/all_gather | solution.py:102
  63.8 11.2 %convolution_convert_fusion = bf16[1024,1536]{1,0:T(8,128)(2,1)} fusion(bf16[1024,2048]{1,0:T(8,128)(2,1)} %all-gather.2.cloned.1.call-done, bf16[2048,1536]{1,0:T(8,128)(2,1)} %param.6), kind=kOutput, calls=%fused_computation.35 | convolution fusion | flops 6444023808 | bytes 13631488 | tf_op jit(solution)/shard_map/dot_general | solution.py:101
  75.0 5.0 reshape.931
  80.0 0.4 slice.83
  80.4 1.2 copy.137
  81.6 3.3 gather_fusion
  85.0 10.9 %all-to-all-start = ((bf16[64,1,128,128]{3,2,1,0:T(8,128)(2,1)}), bf16[64,1,128,128]{3,2,1,0:T(8,128)(2,1)}, u32[]{:S(2)}, u32[]{:S(2)}) async-start(bf16[64,1,128,128]{3,2,1,0:T(8,128)(2,1)} %bitcast.166), calls=%async_computation | async-start | bytes 4194304 | tf_op jit(solution)/shard_map/all_to_all | solution.py:164
  95.9 0.2 fusion.85
  96.0 0.7 copy.160
  96.8 3.5 collective-permute-start
  100.3 0.7 copy.159
  101.1 2.1 collective-permute-start.1
  103.2 0.7 reduce.16
  104.1 0.7 slice.85
  104.8 0.5 copy.106
  105.3 38.3 %collective-permute-done = bf16[128,2,4,128]{3,0,2,1:T(8,128)(2,1)S(1)} collective-permute-done((bf16[128,2,4,128]{3,0,2,1:T(8,128)(2,1)}, bf16[128,2,4,128]{3,0,2,1:T(8,128)(2,1)S(1)}, u32[]{:S(2)}, u32[]{:S(2)}) %collective-permute-start) | collective-permute-done | bytes 262176 | tf_op jit(solution)/shard_map/ppermute | solution.py:15
  143.6 2.4 collective-permute-done.1
  146.0 1.1 pad_maximum_fusion.2
  147.1 0.3 copy.157
  147.5 3.7 fusion.86
  151.4 6.7 gather_fusion.8
  158.0 9.3 %all-to-all-start.3 = ((bf16[64,2,2,128,128]{4,3,2,1,0:T(8,128)(2,1)}), bf16[64,2,2,128,128]{4,3,2,1,0:T(8,128)(2,1)}, u32[]{:S(2)}, u32[]{:S(2)}) async-start(bf16[64,2,2,128,128]{4,3,2,1,0:T(8,128)(2,1)} %bitcast.161), calls=%async_computation.3 | async-start | bytes 16777216 | tf_op jit(solution)/shard_map/all_to_all | solution.py:153
  167.4 1.9 copy.109
  169.2 0.3 copy-done.5
  169.6 0.2 copy.111
  169.8 3.3 pad_maximum_fusion
  173.1 10.0 %gather_fusion.2 = bf16[64,3,2,128,128]{4,3,2,1,0:T(8,128)(2,1)} fusion(bf16[32,3,2,128,128]{4,3,2,0,1:T(8,128)(2,1)} %pad_maximum_fusion, s32[1024]{0:T(1024)S(1)} %pad_clamp_fusion.6), kind=kCustom, calls=%fused_computation.2 | custom fusion | bytes 25166080 | tf_op jit(solution)/shard_map/gather | solution.py:162
  183.1 170.1 %all-to-all-done.3 = bf16[64,2,2,128,128]{4,3,2,1,0:T(8,128)(2,1)} async-done(((bf16[64,2,2,128,128]{4,3,2,1,0:T(8,128)(2,1)}), bf16[64,2,2,128,128]{4,3,2,1,0:T(8,128)(2,1)}, u32[]{:S(2)}, u32[]{:S(2)}) %all-to-all-start.3) | async-done | bytes 8388640 | tf_op jit(solution)/shard_map/all_to_all | solution.py:153
  353.1 6.2 all-to-all-start.1
  359.3 0.3 all-reduce.2.cloned.1.call-start
  359.7 0.8 gather_fusion.5
  361.5 1.7 fusion.37
  363.3 221.0 %all-reduce.2.cloned.1.call-done = bf16[4,2,128,128]{3,2,1,0:T(8,128)(2,1)} async-done(((bf16[4,2,128,128]{3,2,1,0:T(8,128)(2,1)}), bf16[4,2,128,128]{3,2,1,0:T(8,128)(2,1)}) %all-reduce.2.cloned.1.call-update) | async-done | bytes 262160 | tf_op jit(solution)/shard_map/psum | solution.py:25
  584.3 1.9 gather_fusion.4
  586.2 1.5 copy.158
  587.7 2.3 gather_fusion.1
  590.1 1.0 gather_fusion.6
  591.0 10.0 %gather_fusion.9 = bf16[128,2,128,128]{3,2,1,0:T(8,128)(2,1)} fusion(bf16[128,2,128,128]{3,2,1,0:T(8,128)(2,1)} %bitcast.37, s32[1024]{0:T(1024)S(1)} %pad_clamp_fusion.1), kind=kCustom, calls=%fused_computation.9 | custom fusion | bytes 16777728 | tf_op jit(solution)/shard_map/gather | solution.py:154
  601.0 6.4 gather_fusion.10
  607.4 5.2 multiply_reduce_fusion
  612.7 0.4 select_reduce_fusion.1
  613.1 25.2 %all-to-all-done.1 = bf16[64,1,3,2,128,128]{5,4,3,2,1,0:T(8,128)(2,1)} async-done(((bf16[64,1,3,2,128,128]{5,4,3,2,1,0:T(8,128)(2,1)}), bf16[64,1,3,2,128,128]{5,4,3,2,1,0:T(8,128)(2,1)}, u32[]{:S(2)}, u32[]{:S(2)}) %all-to-all-start.1) | async-done | bytes 12582944 | tf_op jit(solution)/shard_map/all_to_all | solution.py:165
  638.3 8.7 %gather_fusion.3 = bf16[32,3,2,128,128]{4,3,2,1,0:T(8,128)(2,1)} fusion(bf16[64,3,2,128,128]{4,3,2,1,0:T(8,128)(2,1)} %bitcast.26, s32[1024]{0:T(1024)S(1)} %pad_clamp_fusion.5), kind=kCustom, calls=%fused_computation.3 | custom fusion | bytes 12583040 | tf_op jit(solution)/shard_map/gather | solution.py:168
  647.0 5.5 fusion
  652.5 0.6 gather_fusion.11
  653.1 3.3 fusion.18
  656.6 2.7 fusion.20
  659.3 0.4 select_reduce_fusion
  659.7 0.9 copy-done.4
  660.6 2.1 fusion.1
  662.7 4.1 fusion.12
  666.8 5.5 fusion.31
  (68 shorter events, 2.5 us)
Async XLA Ops:
  6.5 353.1 %copy-start = (s32[4,512]{1,0:T(4,128)S(1)}, s32[4,512]{1,0:T(4,128)}, u32[]{:S(2)}) copy-start(s32[4,512]{1,0:T(4,128)} %param.9) | copy-start | bytes 24580
  6.5 57.3 %all-gather.2.cloned.1.call-start = ((), (), s32[]{:S(2)}) async-start(), calls=%async_computation.4 | async-start | bytes 5242880 | tf_op jit(solution)/shard_map/all_gather | solution.py:102
  13.3 71.7 %all-to-all-start.2 = ((s32[64,1,2]{2,1,0:T(1,128)}), s32[64,1,2]{2,1,0:T(1,128)S(1)}, u32[]{:S(2)}, u32[]{:S(2)}) async-start(s32[64,1,2]{2,1,0:T(1,128)} %copy.118), calls=%async_computation.2 | async-start | bytes 65536 | tf_op jit(solution)/shard_map/all_to_all | solution.py:151
  85.0 73.1 %all-to-all-start = ((bf16[64,1,128,128]{3,2,1,0:T(8,128)(2,1)}), bf16[64,1,128,128]{3,2,1,0:T(8,128)(2,1)}, u32[]{:S(2)}, u32[]{:S(2)}) async-start(bf16[64,1,128,128]{3,2,1,0:T(8,128)(2,1)} %bitcast.166), calls=%async_computation | async-start | bytes 4194304 | tf_op jit(solution)/shard_map/all_to_all | solution.py:164
  96.8 46.8 %collective-permute-start = (bf16[128,2,4,128]{3,0,2,1:T(8,128)(2,1)}, bf16[128,2,4,128]{3,0,2,1:T(8,128)(2,1)S(1)}, u32[]{:S(2)}, u32[]{:S(2)}) collective-permute-start(bf16[128,2,4,128]{3,0,2,1:T(8,128)(2,1)} %bitcast.157), channel_id=1, source_target_pairs={{0,4},{4,8},{8,12},{12,16},{16,20},{20,24},{24,28},{28,32},{32,36}... | collective-permute-start | bytes 786440 | tf_op jit(solution)/shard_map/ppermute | solution.py:15
  101.1 44.9 %collective-permute-start.1 = (bf16[128,2,4,128]{3,0,2,1:T(8,128)(2,1)}, bf16[128,2,4,128]{3,0,2,1:T(8,128)(2,1)}, u32[]{:S(2)}, u32[]{:S(2)}) collective-permute-start(bf16[128,2,4,128]{3,0,2,1:T(8,128)(2,1)} %bitcast.156), channel_id=1, source_target_pairs={{4,0},{8,4},{12,8},{16,12},{20,16},{24,20},{28,24},{32,28},{36,32}... | collective-permute-start | bytes 786440 | tf_op jit(solution)/shard_map/ppermute | solution.py:18
  147.5 3.8 copy-start.3
  158.0 195.1 %all-to-all-start.3 = ((bf16[64,2,2,128,128]{4,3,2,1,0:T(8,128)(2,1)}), bf16[64,2,2,128,128]{4,3,2,1,0:T(8,128)(2,1)}, u32[]{:S(2)}, u32[]{:S(2)}) async-start(bf16[64,2,2,128,128]{4,3,2,1,0:T(8,128)(2,1)} %bitcast.161), calls=%async_computation.3 | async-start | bytes 16777216 | tf_op jit(solution)/shard_map/all_to_all | solution.py:153
  167.3 2.2 copy-start.5
  353.1 7.9 %copy-start.7 = (s32[32]{0:T(128)S(1)}, s32[32]{0:T(128)}, u32[]{:S(2)}) copy-start(s32[32]{0:T(128)} %get-tuple-element.21) | copy-start | bytes 388
  353.1 285.1 %all-to-all-start.1 = ((bf16[64,1,3,2,128,128]{5,4,3,2,1,0:T(8,128)(2,1)}), bf16[64,1,3,2,128,128]{5,4,3,2,1,0:T(8,128)(2,1)}, u32[]{:S(2)}, u32[]{:S(2)}) async-start(bf16[64,1,3,2,128,128]{5,4,3,2,1,0:T(8,128)(2,1)} %bitcast.160), calls=%async_computation.1 | async-start | bytes 25165824 | tf_op jit(solution)/shard_map/all_to_all | solution.py:165
  359.3 225.0 %all-reduce.2.cloned.1.call-start = ((), (), s32[]{:S(2)}) async-start(), calls=%async_computation.5 | async-start | bytes 524288 | tf_op jit(solution)/shard_map/psum | solution.py:25
  638.3 8.7 %copy-start.6 = (bf16[32,2,128,128]{3,2,0,1:T(8,128)(2,1)S(1)}, bf16[32,2,128,128]{3,2,0,1:T(8,128)(2,1)}, u32[]{:S(2)}) copy-start(bf16[32,2,128,128]{3,2,0,1:T(8,128)(2,1)} %copy.158) | copy-start | bytes 6291460
  653.1 3.4 copy-start.2
  656.6 4.0 copy-start.4
  656.6 10.2 %slice-start = ((s8[6291456]{0:T(1024)(128)(4,1)}), s8[4194304]{0:T(1024)(128)(4,1)S(1)}, s32[]{:S(2)}) async-start(s8[6291456]{0:T(1024)(128)(4,1)} %bitcast.170), calls=%async_computation.6 | async-start | bytes 8388608
  660.6 6.2 slice-start.1
  666.8 5.5 copy-start.1
Sparse Core Ops, SparseCore 0:
  9.2 54.5 all-gather.1
  363.6 220.6 all-reduce.1
where the time goes:
time: 680 us; the launch traced here: 679 us
  waiting for transfers between devices  494 us (73%)
  local copies, waits for them, and re-layouts  75.2 us (11%)
  starting transfers between devices  45.3 us (7%)
  matrix products  34.2 us (5%)
  other arithmetic  16.5 us (2%)
  between operations  13.8 us (2%)
    psum x1, waiting for transfers between devices, broadcast(): return lax.psum(block, axis)  221 us
    all_to_all x1, waiting for transfers between devices, local(): lax.all_to_all(picked, 'seq', split_axis=0, concat_axis=0, tiled=True)  170 us
    ppermute x1, waiting for transfers between devices, extended(): lax.ppermute(lax.slice_in_dim(block, block.shape[dim] - width, None, axis...  38.3 us
    all_gather x1, waiting for transfers between devices, local(): lax.all_gather(tokens, 'head', axis=1, tiled=True)  36.4 us
    all_to_all x1, waiting for transfers between devices, local(): lax.all_to_all(sent_window, 'seq', split_axis=0, concat_axis=0, tiled=True)  25.2 us
  transfers between devices with their start and end apart: 8, of which 6 were waited for; matrix products, arithmetic and copies ran while one was open for 14% of the time, Pallas kernels for 0%

commit v1 on v0

--- a/solution.py
+++ b/solution.py
@@ -99,7 +99,10 @@
     cap_tiles = max(1, slot_count // seq_count)
     factor = 1.0 / math.sqrt(head_dim)
     projected = jnp.dot(
-        lax.all_gather(tokens, "head", axis=1, tiled=True),
+        jnp.concatenate(
+            lax.all_to_all(jnp.stack([tokens for _ in range(lax.axis_size("head"))]), "head", 0, 0),
+            1,
+        ),
         w_qkv,
         preferred_element_type=jnp.float32,
     )

time: 680 us -> 694 us (1.021)
    all_to_all x0 -> x1, waiting for transfers between devices: none -> 42 us  [local(): lax.all_to_all(jnp.stack([tokens for _ in range(lax.axis_size('head'))]),...]
    all_gather x1 -> x0, waiting for transfers between devices: 36.4 us -> none  [local(): lax.all_gather(tokens, 'head', axis=1, tiled=True)]
  transfers between devices with their start and end apart: 8 -> 8, of which waited for: 6 -> 6; matrix products, arithmetic and copies ran while one was open for 14% -> 13% of each run, Pallas kernels for 0% -> 0%
where the time goes in v1:
time: 694 us; the launch traced here: 693 us
  waiting for transfers between devices  499 us (72%)
  local copies, waits for them, and re-layouts  77.8 us (11%)
  starting transfers between devices  51.9 us (7%)
  matrix products  34.5 us (5%)
  other arithmetic  15.8 us (2%)
  between operations  13.8 us (2%)
    psum x1, waiting for transfers between devices, broadcast(): return lax.psum(block, axis)  222 us
    all_to_all x1, waiting for transfers between devices, local(): lax.all_to_all(picked, 'seq', split_axis=0, concat_axis=0, tiled=True)  170 us
    all_to_all x1, waiting for transfers between devices, local(): lax.all_to_all(jnp.stack([tokens for _ in range(lax.axis_size('head'))]),...  42 us
    ppermute x1, waiting for transfers between devices, extended(): lax.ppermute(lax.slice_in_dim(block, block.shape[dim] - width, None, axis...  38.3 us
    all_to_all x1, waiting for transfers between devices, local(): lax.all_to_all(sent_window, 'seq', split_axis=0, concat_axis=0, tiled=True)  24.5 us
    all_to_all x1, starting transfers between devices, local(): lax.all_to_all(requests, 'seq', split_axis=0, concat_axis=0, tiled=True)  14.9 us
  transfers between devices with their start and end apart: 8, of which 6 were waited for; matrix products, arithmetic and copies ran while one was open for 13% of the time, Pallas kernels for 0%

profile of v1, /device:TPU:1, one launch (start us, length us, event | category | flops | bytes accessed | tf_op | source)
XLA Modules:
  0.0 692.9 jit_solution(15917607779844787802)
XLA Ops:
  6.5 1.5 copy.106
  8.0 2.5 stack.19
  10.6 5.1 all-to-all-start
  15.7 0.5 broadcast.1182
  16.3 0.6 reduce.15
  17.0 0.2 reduce_window_sum.18
  17.3 0.4 copy.121
  17.7 0.2 convert_reduce_fusion.1
  17.9 0.6 fusion.78
  18.5 0.7 gather_fusion.7
  19.9 0.7 copy.122
  20.8 42.0 %all-to-all-done = bf16[4,1024,512]{1,2,0:T(8,128)(2,1)} async-done(((bf16[4,1024,512]{1,2,0:T(8,128)(2,1)}), bf16[4,1024,512]{1,2,0:T(8,128)(2,1)}, u32[]{:S(2)}, u32[]{:S(2)}) %all-to-all-start) | async-done | bytes 4194336 | tf_op jit(solution)/shard_map/all_to_all | solution.py:103
  62.8 14.9 %all-to-all-start.3 = ((s32[64,1,2]{2,1,0:T(1,128)}), s32[64,1,2]{2,1,0:T(1,128)S(1)}, u32[]{:S(2)}, u32[]{:S(2)}) async-start(s32[64,1,2]{2,1,0:T(1,128)} %copy.122), calls=%async_computation.3 | async-start | bytes 65536 | tf_op jit(solution)/shard_map/all_to_all | solution.py:154
  77.7 11.5 %convolution_convert_fusion = bf16[1024,1536]{1,0:T(8,128)(2,1)} fusion(bf16[1024,2048]{0,1:T(8,128)(2,1)} %bitcast.2, bf16[2048,1536]{1,0:T(8,128)(2,1)} %param.6), kind=kOutput, calls=%fused_computation.35 | convolution fusion | flops 6444023808 | bytes 13631488 | tf_op jit(solution)/shard_map/dot_general | solution.py:101
  89.2 5.0 reshape.941
  94.2 0.4 slice.83
  94.5 1.2 copy.141
  95.8 3.3 gather_fusion
  99.1 10.5 %all-to-all-start.1 = ((bf16[64,1,128,128]{3,2,1,0:T(8,128)(2,1)}), bf16[64,1,128,128]{3,2,1,0:T(8,128)(2,1)}, u32[]{:S(2)}, u32[]{:S(2)}) async-start(bf16[64,1,128,128]{3,2,1,0:T(8,128)(2,1)} %bitcast.169), calls=%async_computation.1 | async-start | bytes 4194304 | tf_op jit(solution)/shard_map/all_to_all | solution.py:167
  109.6 0.2 fusion.85
  109.8 0.7 copy.164
  110.6 3.5 collective-permute-start
  114.1 0.7 copy.163
  114.8 2.1 collective-permute-start.1
  116.9 0.7 reduce.16
  117.8 0.7 slice.85
  118.6 0.5 copy.110
  119.1 38.3 %collective-permute-done = bf16[128,2,4,128]{3,0,2,1:T(8,128)(2,1)S(1)} collective-permute-done((bf16[128,2,4,128]{3,0,2,1:T(8,128)(2,1)}, bf16[128,2,4,128]{3,0,2,1:T(8,128)(2,1)S(1)}, u32[]{:S(2)}, u32[]{:S(2)}) %collective-permute-start) | collective-permute-done | bytes 262176 | tf_op jit(solution)/shard_map/ppermute | solution.py:15
  157.3 2.4 collective-permute-done.1
  159.8 1.1 pad_maximum_fusion.2
  160.9 0.3 copy.161
  161.2 3.7 fusion.86
  165.1 6.7 gather_fusion.8
  171.8 9.3 %all-to-all-start.4 = ((bf16[64,2,2,128,128]{4,3,2,1,0:T(8,128)(2,1)}), bf16[64,2,2,128,128]{4,3,2,1,0:T(8,128)(2,1)}, u32[]{:S(2)}, u32[]{:S(2)}) async-start(bf16[64,2,2,128,128]{4,3,2,1,0:T(8,128)(2,1)} %bitcast.164), calls=%async_computation.4 | async-start | bytes 16777216 | tf_op jit(solution)/shard_map/all_to_all | solution.py:156
  181.1 1.9 copy.113
  183.0 0.3 copy-done.5
  183.3 0.2 copy.115
  183.6 3.3 pad_maximum_fusion
  186.8 10.0 %gather_fusion.2 = bf16[64,3,2,128,128]{4,3,2,1,0:T(8,128)(2,1)} fusion(bf16[32,3,2,128,128]{4,3,2,0,1:T(8,128)(2,1)} %pad_maximum_fusion, s32[1024]{0:T(1024)S(1)} %pad_clamp_fusion.6), kind=kCustom, calls=%fused_computation.2 | custom fusion | bytes 25166080 | tf_op jit(solution)/shard_map/gather | solution.py:165
  196.8 170.1 %all-to-all-done.4 = bf16[64,2,2,128,128]{4,3,2,1,0:T(8,128)(2,1)} async-done(((bf16[64,2,2,128,128]{4,3,2,1,0:T(8,128)(2,1)}), bf16[64,2,2,128,128]{4,3,2,1,0:T(8,128)(2,1)}, u32[]{:S(2)}, u32[]{:S(2)}) %all-to-all-start.4) | async-done | bytes 8388640 | tf_op jit(solution)/shard_map/all_to_all | solution.py:156
  366.9 6.2 all-to-all-start.2
  373.1 0.3 all-reduce.2.cloned.1.call-start
  373.4 0.8 gather_fusion.5
  375.3 1.7 fusion.37
  377.1 221.7 %all-reduce.2.cloned.1.call-done = bf16[4,2,128,128]{3,2,1,0:T(8,128)(2,1)} async-done(((bf16[4,2,128,128]{3,2,1,0:T(8,128)(2,1)}), bf16[4,2,128,128]{3,2,1,0:T(8,128)(2,1)}) %all-reduce.2.cloned.1.call-update) | async-done | bytes 262160 | tf_op jit(solution)/shard_map/psum | solution.py:25
  598.8 1.9 gather_fusion.4
  600.7 1.5 copy.162
  602.2 2.3 gather_fusion.1
  604.5 1.0 gather_fusion.6
  605.5 10.0 %gather_fusion.9 = bf16[128,2,128,128]{3,2,1,0:T(8,128)(2,1)} fusion(bf16[128,2,128,128]{3,2,1,0:T(8,128)(2,1)} %bitcast.39, s32[1024]{0:T(1024)S(1)} %pad_clamp_fusion.1), kind=kCustom, calls=%fused_computation.9 | custom fusion | bytes 16777728 | tf_op jit(solution)/shard_map/gather | solution.py:157
  615.5 6.4 gather_fusion.10
  621.9 5.2 multiply_reduce_fusion
  627.1 0.4 select_reduce_fusion.1
  627.5 24.5 %all-to-all-done.2 = bf16[64,1,3,2,128,128]{5,4,3,2,1,0:T(8,128)(2,1)} async-done(((bf16[64,1,3,2,128,128]{5,4,3,2,1,0:T(8,128)(2,1)}), bf16[64,1,3,2,128,128]{5,4,3,2,1,0:T(8,128)(2,1)}, u32[]{:S(2)}, u32[]{:S(2)}) %all-to-all-start.2) | async-done | bytes 12582944 | tf_op jit(solution)/shard_map/all_to_all | solution.py:168
  652.0 8.7 %gather_fusion.3 = bf16[32,3,2,128,128]{4,3,2,1,0:T(8,128)(2,1)} fusion(bf16[64,3,2,128,128]{4,3,2,1,0:T(8,128)(2,1)} %bitcast.28, s32[1024]{0:T(1024)S(1)} %pad_clamp_fusion.5), kind=kCustom, calls=%fused_computation.3 | custom fusion | bytes 12583040 | tf_op jit(solution)/shard_map/gather | solution.py:171
  660.8 5.5 fusion
  666.3 0.6 gather_fusion.11
  666.9 3.3 fusion.18
  670.3 2.7 fusion.20
  673.1 0.4 select_reduce_fusion
  673.4 0.9 copy-done.4
  674.3 2.1 fusion.1
  676.5 4.1 fusion.12
  680.6 5.5 fusion.31
  (73 shorter events, 2.8 us)
Async XLA Ops:
  6.5 366.9 %copy-start = (s32[4,512]{1,0:T(4,128)S(1)}, s32[4,512]{1,0:T(4,128)}, u32[]{:S(2)}) copy-start(s32[4,512]{1,0:T(4,128)} %param.9) | copy-start | bytes 24580
  10.6 5.7 copy-start.8
  10.6 6.7 copy-start.7
  10.6 52.2 %all-to-all-start = ((bf16[4,1024,512]{1,2,0:T(8,128)(2,1)}), bf16[4,1024,512]{1,2,0:T(8,128)(2,1)}, u32[]{:S(2)}, u32[]{:S(2)}) async-start(bf16[4,1024,512]{1,2,0:T(8,128)(2,1)} %stack.19), calls=%async_computation | async-start | bytes 8388608 | tf_op jit(solution)/shard_map/all_to_all | solution.py:103
  62.8 36.3 %all-to-all-start.3 = ((s32[64,1,2]{2,1,0:T(1,128)}), s32[64,1,2]{2,1,0:T(1,128)S(1)}, u32[]{:S(2)}, u32[]{:S(2)}) async-start(s32[64,1,2]{2,1,0:T(1,128)} %copy.122), calls=%async_computation.3 | async-start | bytes 65536 | tf_op jit(solution)/shard_map/all_to_all | solution.py:154
  99.1 72.7 %all-to-all-start.1 = ((bf16[64,1,128,128]{3,2,1,0:T(8,128)(2,1)}), bf16[64,1,128,128]{3,2,1,0:T(8,128)(2,1)}, u32[]{:S(2)}, u32[]{:S(2)}) async-start(bf16[64,1,128,128]{3,2,1,0:T(8,128)(2,1)} %bitcast.169), calls=%async_computation.1 | async-start | bytes 4194304 | tf_op jit(solution)/shard_map/all_to_all | solution.py:167
  110.6 46.8 %collective-permute-start = (bf16[128,2,4,128]{3,0,2,1:T(8,128)(2,1)}, bf16[128,2,4,128]{3,0,2,1:T(8,128)(2,1)S(1)}, u32[]{:S(2)}, u32[]{:S(2)}) collective-permute-start(bf16[128,2,4,128]{3,0,2,1:T(8,128)(2,1)} %bitcast.160), channel_id=1, source_target_pairs={{0,4},{4,8},{8,12},{12,16},{16,20},{20,24},{24,28},{28,32},{32,36}... | collective-permute-start | bytes 786440 | tf_op jit(solution)/shard_map/ppermute | solution.py:15
  114.8 44.9 %collective-permute-start.1 = (bf16[128,2,4,128]{3,0,2,1:T(8,128)(2,1)}, bf16[128,2,4,128]{3,0,2,1:T(8,128)(2,1)}, u32[]{:S(2)}, u32[]{:S(2)}) collective-permute-start(bf16[128,2,4,128]{3,0,2,1:T(8,128)(2,1)} %bitcast.159), channel_id=1, source_target_pairs={{4,0},{8,4},{12,8},{16,12},{20,16},{24,20},{28,24},{32,28},{36,32}... | collective-permute-start | bytes 786440 | tf_op jit(solution)/shard_map/ppermute | solution.py:18
  161.2 3.8 copy-start.3
  171.8 195.1 %all-to-all-start.4 = ((bf16[64,2,2,128,128]{4,3,2,1,0:T(8,128)(2,1)}), bf16[64,2,2,128,128]{4,3,2,1,0:T(8,128)(2,1)}, u32[]{:S(2)}, u32[]{:S(2)}) async-start(bf16[64,2,2,128,128]{4,3,2,1,0:T(8,128)(2,1)} %bitcast.164), calls=%async_computation.4 | async-start | bytes 16777216 | tf_op jit(solution)/shard_map/all_to_all | solution.py:156
  181.1 2.2 copy-start.5
  366.9 7.9 %copy-start.9 = (s32[32]{0:T(128)S(1)}, s32[32]{0:T(128)}, u32[]{:S(2)}) copy-start(s32[32]{0:T(128)} %get-tuple-element.21) | copy-start | bytes 388
  366.9 285.1 %all-to-all-start.2 = ((bf16[64,1,3,2,128,128]{5,4,3,2,1,0:T(8,128)(2,1)}), bf16[64,1,3,2,128,128]{5,4,3,2,1,0:T(8,128)(2,1)}, u32[]{:S(2)}, u32[]{:S(2)}) async-start(bf16[64,1,3,2,128,128]{5,4,3,2,1,0:T(8,128)(2,1)} %bitcast.163), calls=%async_computation.2 | async-start | bytes 25165824 | tf_op jit(solution)/shard_map/all_to_all | solution.py:168
  373.1 225.7 %all-reduce.2.cloned.1.call-start = ((), (), s32[]{:S(2)}) async-start(), calls=%async_computation.5 | async-start | bytes 524288 | tf_op jit(solution)/shard_map/psum | solution.py:25
  652.0 8.7 %copy-start.6 = (bf16[32,2,128,128]{3,2,0,1:T(8,128)(2,1)S(1)}, bf16[32,2,128,128]{3,2,0,1:T(8,128)(2,1)}, u32[]{:S(2)}) copy-start(bf16[32,2,128,128]{3,2,0,1:T(8,128)(2,1)} %copy.162) | copy-start | bytes 6291460
  666.9 3.4 copy-start.2
  670.3 4.0 copy-start.4
  670.3 10.2 %slice-start = ((s8[6291456]{0:T(1024)(128)(4,1)}), s8[4194304]{0:T(1024)(128)(4,1)S(1)}, s32[]{:S(2)}) async-start(s8[6291456]{0:T(1024)(128)(4,1)} %bitcast.173), calls=%async_computation.6 | async-start | bytes 8388608
  674.3 6.2 slice-start.1
  680.6 5.5 copy-start.1
Sparse Core Ops, SparseCore 0:
  377.4 221.3 all-reduce.1
